TPU v7x, 32 devices: a whole 2x2x4 slice. The times are simulated.
32 devices in a mesh: ctx: 16 (over z, y, x), wsh: 2 (over core).
Axes of the slice: x: 2, y: 2, z: 4, core: 2. Of those that a mesh axis runs over, the one named last changes fastest.
Arguments:
- tokens: bfloat16 [8, 2048, 512], P('wsh', 'ctx'), may hold values from -6 to 6
- routes: int32 [8, 2048, 2], P('wsh', 'ctx'), may hold values from 0 to 7, all different within a row
- block_order: int32 [16], replicated, may hold values from 0 to 15, each once
- norm_gain1: bfloat16 [512], P('wsh'), may hold values from 0.5 to 1.5
- router_w: bfloat16 [512, 8], P('wsh'), may hold values from -0.1875 to 0.1875
- query_w: bfloat16 [512, 512], P('wsh'), may hold values from -0.25 to 0.25
- kv_w: bfloat16 [512, 128], P('wsh'), may hold values from -0.25 to 0.25
- out_w: bfloat16 [512, 512], P('wsh'), may hold values from -6 to 6
- norm_gain2: bfloat16 [512], P('wsh'), may hold values from 0.5 to 1.5
- up_w: bfloat16 [512, 2048], P('wsh'), may hold values from -0.25 to 0.25
- down_w: bfloat16 [2048, 512], P('wsh'), may hold values from -0.125 to 0.125
- cotangent: bfloat16 [8, 2048, 512], P('wsh', 'ctx'), may hold values from -6 to 6
Outputs:
- layer_out: float32 [8, 2048, 512], P('wsh', 'ctx')
- input_grad: float32 [8, 2048, 512], P('wsh', 'ctx')
- grad_gain1: float32 [512], P('wsh')
- grad_router: float32 [512, 8], P('wsh')
- grad_query: float32 [512, 512], P('wsh')
- grad_kv: float32 [512, 128], P('wsh')
- grad_out: float32 [512, 512], P('wsh')
- grad_gain2: float32 [512], P('wsh')
- grad_up: float32 [512, 2048], P('wsh')
- grad_down: float32 [2048, 512], P('wsh')
Inputs may be any that keep to these rules, and one draw needn't show every extreme that they name: `routes`: each token names 2 different experts. A permutation: index p of ctx holds, of every sequence, block block_order[p] and block 31 - block_order[p], as the first step says.
All inputs are finite; a program needn't handle non-finite values.
Results may differ from a plain program's by a relative error of at most 0.013.
Values may be sent and summed in bfloat16 or wider, within the bound.
No kernel may reach another device: no remote copies, remote signals or barrier semaphores. Data moves between devices by JAX's collectives and lax.ppermute only.
A program may use at most 192 MiB of HBM per device.

v0:
```python
import math
import jax
import jax.numpy as jnp
from jax import lax
from jax.sharding import PartitionSpec as P

MB = 4
HIGHEST = lax.Precision.HIGHEST


def smooth_unit(values_in):
    return jax.nn.gelu(values_in, approximate=False)


def normalize(inputs, gain_vec):
    centre = inputs - jnp.mean(inputs, axis=-1, keepdims=True)
    spread = jnp.mean(centre * centre, axis=-1, keepdims=True)
    return centre * lax.rsqrt(spread + 1e-05) * gain_vec


def gating(logits, expert_hot):
    chosen = jnp.sum(expert_hot * logits[..., None, :], axis=-1)
    return jax.nn.softmax(chosen, axis=-1)


def tile_scores(queries, kv_all, query_places, key_places, first_row, width):
    head = queries.shape[-1]
    tile = lax.dynamic_slice_in_dim(kv_all, first_row, width, 1)
    places = lax.dynamic_slice_in_dim(key_places, first_row, width, 0)
    keys_tile = tile[..., :head]
    values_tile = tile[..., head:]
    scores = jnp.einsum("btsh,bkh->btsk", queries, keys_tile, preferred_element_type=jnp.float32)
    allowed = places[None, None, None, :] <= query_places[None, :, None, None]
    return (keys_tile, values_tile, scores, allowed)


def log_totals(queries, kv_all, query_places, key_places):
    rows = kv_all.shape[1]
    width = math.gcd(rows, 2048)

    def log_advance(carry, index):
        top_score, total = carry
        unused_keys, unused_values, scores, allowed = tile_scores(
            queries, kv_all, query_places, key_places, index * width, width
        )
        fresh = jnp.maximum(top_score, jnp.max(jnp.where(allowed, scores, -1e30), axis=-1))
        shares = jnp.where(allowed, jnp.exp(scores - fresh[..., None]), 0.0)
        total = total * jnp.exp(top_score - fresh) + jnp.sum(shares, axis=-1)
        return ((fresh, total), None)

    shape = queries.shape[:-1]
    initial = (jnp.full(shape, -1e30, jnp.float32), jnp.zeros(shape, jnp.float32))
    carry, unused = lax.scan(log_advance, initial, jnp.arange(rows // width, dtype=jnp.int32))
    return carry[0] + jnp.log(carry[1])


def attend(queries, kv_all, query_places, key_places, log_total):
    rows = kv_all.shape[1]
    width = math.gcd(rows, 2048)

    def attend_advance(carry, index):
        unused_keys, values_tile, scores, allowed = tile_scores(
            queries, kv_all, query_places, key_places, index * width, width
        )
        shares = jnp.where(allowed, jnp.exp(scores - log_total[..., None]), 0.0).astype(
            jnp.bfloat16
        )
        return (
            carry
            + jnp.einsum("btsk,bkh->btsh", shares, values_tile, preferred_element_type=jnp.float32),
            None,
        )

    summed, unused = lax.scan(
        attend_advance,
        jnp.zeros(queries.shape, jnp.float32),
        jnp.arange(rows // width, dtype=jnp.int32),
    )
    return summed


def key_range_grads(
    queries, back_attended, kv_all, query_places, key_places, log_total, row_delta, begin, row_count
):
    width = math.gcd(row_count, 2048)

    def key_advance(carry, index):
        back_query, back_kv = carry
        keys_tile, values_tile, scores, allowed = tile_scores(
            queries, kv_all, query_places, key_places, begin + index * width, width
        )
        shares = jnp.where(allowed, jnp.exp(scores - log_total[..., None]), 0.0)
        back_shares = jnp.einsum(
            "btsh,bkh->btsk", back_attended, values_tile, preferred_element_type=jnp.float32
        )
        back_scores = (shares * (back_shares - row_delta[..., None])).astype(jnp.bfloat16)
        back_query = back_query + jnp.einsum(
            "btsk,bkh->btsh", back_scores, keys_tile, preferred_element_type=jnp.float32
        )
        back_keys = jnp.einsum(
            "btsk,btsh->bkh", back_scores, queries, preferred_element_type=jnp.float32
        )
        back_values = jnp.einsum(
            "btsk,btsh->bkh",
            shares.astype(jnp.bfloat16),
            back_attended,
            preferred_element_type=jnp.float32,
        )
        back_kv = lax.dynamic_update_slice_in_dim(
            back_kv, jnp.concatenate([back_keys, back_values], axis=-1), index * width, 1
        )
        return ((back_query, back_kv), None)

    head = queries.shape[-1]
    kv_start = jnp.zeros((queries.shape[0], row_count, 2 * head), jnp.float32)
    carry, unused = lax.scan(
        key_advance,
        (jnp.zeros(queries.shape, jnp.float32), kv_start),
        jnp.arange(row_count // width, dtype=jnp.int32),
    )
    return carry


def on_device(
    tokens,
    routes,
    block_order,
    norm_gain1,
    router_w,
    query_w,
    kv_w,
    out_w,
    norm_gain2,
    up_w,
    down_w,
    cotangent,
):
    gathered = (
        lax.all_gather(norm_gain1, "wsh", axis=0, tiled=True),
        lax.all_gather(router_w, "wsh", axis=0, tiled=True),
        lax.all_gather(query_w, "wsh", axis=0, tiled=True),
        lax.all_gather(kv_w, "wsh", axis=0, tiled=True),
        lax.all_gather(out_w, "wsh", axis=0, tiled=True),
        lax.all_gather(norm_gain2, "wsh", axis=0, tiled=True),
        lax.all_gather(up_w, "wsh", axis=0, tiled=True),
        lax.all_gather(down_w, "wsh", axis=0, tiled=True),
    )
    gain_one, router, query_mat, kv_mat, out_mat, gain_two, up_mat, down_mat = gathered
    gain_one_f = gain_one.astype(jnp.float32)
    gain_two_f = gain_two.astype(jnp.float32)
    router_f = router.astype(jnp.float32)
    experts = router.shape[1]
    head = kv_mat.shape[1] // 2
    pairs = lax.axis_size("ctx")
    local = tokens.shape[1]
    block = local // 2
    offsets = jnp.arange(block, dtype=jnp.int32)
    front_rows = block_order[:, None] * block + offsets[None, :]
    back_rows = (2 * pairs - 1 - block_order)[:, None] * block + offsets[None, :]
    key_places = jnp.concatenate([front_rows, back_rows], axis=1).reshape(-1)
    length = key_places.shape[0]
    query_places = lax.dynamic_slice_in_dim(key_places, lax.axis_index("ctx") * local, local, 0)
    group = tokens.shape[0] // MB
    totals = [jnp.zeros(w.shape, jnp.float32) for w in gathered]
    layer_parts = []
    input_parts = []
    for batch in range(MB):
        inputs = tokens[batch * group : (batch + 1) * group].astype(jnp.float32)
        seq_routes = routes[batch * group : (batch + 1) * group]
        seq_cotangent = cotangent[batch * group : (batch + 1) * group]
        seqs = inputs.shape[0]
        expert_hot = (seq_routes[..., None] == jnp.arange(experts, dtype=jnp.int32)).astype(
            jnp.float32
        )
        normed, norm_pull_one = jax.vjp(normalize, inputs, gain_one_f)
        normed_low = normed.astype(jnp.bfloat16)
        logits = jnp.dot(normed_low, router, preferred_element_type=jnp.float32)
        gate_values, gate_pull = jax.vjp(lambda values_in: gating(values_in, expert_hot), logits)
        query_all = jnp.dot(normed_low, query_mat, preferred_element_type=jnp.float32).reshape(
            seqs, local, experts, head
        )
        queries = (
            jnp.einsum("btse,bteh->btsh", expert_hot, query_all, precision=HIGHEST) * 0.125
        ).astype(jnp.bfloat16)
        keyval = jnp.dot(normed_low, kv_mat, preferred_element_type=jnp.float32).astype(
            jnp.bfloat16
        )
        kv_all = lax.all_gather(keyval, "ctx", axis=1, tiled=True)
        log_total = log_totals(queries, kv_all, query_places, key_places)
        attended = attend(queries, kv_all, query_places, key_places, log_total)
        weighted = gate_values[..., None] * attended
        mixed_heads = (
            jnp.einsum("btse,btsh->bteh", expert_hot, weighted, precision=HIGHEST)
            .reshape(seqs, local, experts * head)
            .astype(jnp.bfloat16)
        )
        hidden = inputs + jnp.dot(mixed_heads, out_mat, preferred_element_type=jnp.float32)
        normed_two, norm_pull_two = jax.vjp(normalize, hidden, gain_two_f)
        normed_two_low = normed_two.astype(jnp.bfloat16)
        pre_act = jnp.dot(normed_two_low, up_mat, preferred_element_type=jnp.float32)
        act_values, act_pull = jax.vjp(smooth_unit, pre_act)
        activated = act_values.astype(jnp.bfloat16)
        layer_parts.append(
            hidden + jnp.dot(activated, down_mat, preferred_element_type=jnp.float32)
        )
        totals[7] = totals[7] + jnp.einsum(
            "btf,btd->fd", activated, seq_cotangent, preferred_element_type=jnp.float32
        )
        back_act = jnp.einsum(
            "btd,fd->btf", seq_cotangent, down_mat, preferred_element_type=jnp.float32
        )
        (back_pre_f,) = act_pull(back_act)
        back_pre = back_pre_f.astype(jnp.bfloat16)
        totals[6] = totals[6] + jnp.einsum(
            "btd,btf->df", normed_two_low, back_pre, preferred_element_type=jnp.float32
        )
        back_normed_two = jnp.einsum(
            "btf,df->btd", back_pre, up_mat, preferred_element_type=jnp.float32
        )
        hidden_part, gain_two_grad = norm_pull_two(back_normed_two)
        back_hidden = seq_cotangent.astype(jnp.float32) + hidden_part
        totals[5] = totals[5] + gain_two_grad
        back_branch = back_hidden.astype(jnp.bfloat16)
        totals[4] = totals[4] + jnp.einsum(
            "btk,btd->kd", mixed_heads, back_branch, preferred_element_type=jnp.float32
        )
        back_mixed = jnp.einsum(
            "btd,kd->btk", back_branch, out_mat, preferred_element_type=jnp.float32
        ).reshape(seqs, local, experts, head)
        back_slots = jnp.einsum("btse,bteh->btsh", expert_hot, back_mixed, precision=HIGHEST)
        back_gates = jnp.sum(back_slots * attended, axis=-1)
        back_attended = (gate_values[..., None] * back_slots).astype(jnp.bfloat16)
        row_delta = jnp.sum(back_attended.astype(jnp.float32) * attended, axis=-1)
        (back_logits,) = gate_pull(back_gates)
        back_query, full_kv = key_range_grads(
            queries,
            back_attended,
            kv_all,
            query_places,
            key_places,
            log_total,
            row_delta,
            0,
            length,
        )
        own_kv = lax.psum_scatter(full_kv, "ctx", scatter_dimension=1, tiled=True)
        back_kv_low = own_kv.astype(jnp.bfloat16)
        back_query_low = back_query.astype(jnp.bfloat16)
        back_qall = (
            (
                jnp.einsum(
                    "btse,btsh->bteh",
                    expert_hot.astype(jnp.bfloat16),
                    back_query_low,
                    preferred_element_type=jnp.float32,
                )
                * 0.125
            )
            .reshape(seqs, local, experts * head)
            .astype(jnp.bfloat16)
        )
        totals[2] = totals[2] + jnp.einsum(
            "btd,btk->dk", normed_low, back_qall, preferred_element_type=jnp.float32
        )
        totals[3] = totals[3] + jnp.einsum(
            "btd,btk->dk", normed_low, back_kv_low, preferred_element_type=jnp.float32
        )
        totals[1] = totals[1] + jnp.einsum(
            "btd,bte->de", normed_low.astype(jnp.float32), back_logits, precision=HIGHEST
        )
        back_normed = jnp.einsum(
            "btk,dk->btd", back_qall, query_mat, preferred_element_type=jnp.float32
        )
        back_normed = back_normed + jnp.einsum(
            "btk,dk->btd", back_kv_low, kv_mat, preferred_element_type=jnp.float32
        )
        back_normed = back_normed + jnp.einsum(
            "bte,de->btd", back_logits, router_f, precision=HIGHEST
        )
        input_part, gain_one_grad = norm_pull_one(back_normed)
        totals[0] = totals[0] + gain_one_grad
        input_parts.append(back_hidden + input_part)
    layer_out = jnp.concatenate(layer_parts, axis=0)
    input_grad = jnp.concatenate(input_parts, axis=0)
    owned = (
        lax.psum_scatter(
            totals[0].astype(jnp.bfloat16), "wsh", scatter_dimension=0, tiled=True
        ).astype(jnp.float32),
        lax.psum_scatter(
            totals[1].astype(jnp.bfloat16), "wsh", scatter_dimension=0, tiled=True
        ).astype(jnp.float32),
        lax.psum_scatter(
            totals[2].astype(jnp.bfloat16), "wsh", scatter_dimension=0, tiled=True
        ).astype(jnp.float32),
        lax.psum_scatter(
            totals[3].astype(jnp.bfloat16), "wsh", scatter_dimension=0, tiled=True
        ).astype(jnp.float32),
        lax.psum_scatter(
            totals[4].astype(jnp.bfloat16), "wsh", scatter_dimension=0, tiled=True
        ).astype(jnp.float32),
        lax.psum_scatter(
            totals[5].astype(jnp.bfloat16), "wsh", scatter_dimension=0, tiled=True
        ).astype(jnp.float32),
        lax.psum_scatter(
            totals[6].astype(jnp.bfloat16), "wsh", scatter_dimension=0, tiled=True
        ).astype(jnp.float32),
        lax.psum_scatter(
            totals[7].astype(jnp.bfloat16), "wsh", scatter_dimension=0, tiled=True
        ).astype(jnp.float32),
    )
    summed = lax.psum(
        (owned[0], owned[1], owned[2], owned[3], owned[4], owned[5], owned[6], owned[7]), "ctx"
    )
    return (
        layer_out,
        input_grad,
        summed[0],
        summed[1],
        summed[2],
        summed[3],
        summed[4],
        summed[5],
        summed[6],
        summed[7],
    )


def solution(mesh):
    placed = (
        P("wsh", "ctx", None),
        P("wsh", "ctx", None),
        P(),
        P("wsh"),
        P("wsh", None),
        P("wsh", None),
        P("wsh", None),
        P("wsh", None),
        P("wsh"),
        P("wsh", None),
        P("wsh", None),
        P("wsh", "ctx", None),
    )
    return jax.shard_map(
        on_device,
        mesh=mesh,
        in_specs=placed,
        out_specs=(
            P("wsh", "ctx", None),
            P("wsh", "ctx", None),
            P("wsh"),
            P("wsh", None),
            P("wsh", None),
            P("wsh", None),
            P("wsh", None),
            P("wsh"),
            P("wsh", None),
            P("wsh", None),
        ),
        check_vma=False,
    )
```

profile of v0, /device:TPU:0, one launch (start us, length us, event | category | flops | bytes accessed | tf_op | source)
XLA Modules:
  0.0 953.8 jit_solution(5892758774405874934)
XLA Ops:
  20.5 2.6 all_gather.38
  30.5 45.1 %all-gather.3 = bf16[2048,128]{1,0:T(8,128)(2,1)S(1)} all-gather(bf16[128,128]{1,0:T(8,128)(2,1)S(1)} %convolution_convert_fusion.8), channel_id=5, replica_groups=mesh['ctx'=16,'wsh'=2] {'ctx'}, dimensions={0}, use_global_device_ids=true | all-gather | bytes 557056 | tf_op jit(solution)/shard_map/all_gather | solution.py:188
  75.7 38.7 %all-gather.2 = bf16[2048,128]{1,0:T(8,128)(2,1)S(1)} all-gather(bf16[128,128]{1,0:T(8,128)(2,1)S(1)} %convolution_convert_fusion.9), channel_id=4, replica_groups=mesh['ctx'=16,'wsh'=2] {'ctx'}, dimensions={0}, use_global_device_ids=true | all-gather | bytes 557056 | tf_op jit(solution)/shard_map/all_gather | solution.py:188
  114.3 40.8 %all-gather.1 = bf16[2048,128]{1,0:T(8,128)(2,1)S(1)} all-gather(bf16[128,128]{1,0:T(8,128)(2,1)S(1)} %convolution_convert_fusion.10), channel_id=3, replica_groups=mesh['ctx'=16,'wsh'=2] {'ctx'}, dimensions={0}, use_global_device_ids=true | all-gather | bytes 557056 | tf_op jit(solution)/shard_map/all_gather | solution.py:188
  155.1 2.4 all_gather.41
  167.1 3.2 broadcast_multiply_fusion.1
  171.9 2.6 convolution_convert_fusion.1
  176.3 2.5 broadcast_multiply_fusion.2
  184.3 2.0 all-gather.5
  189.0 5.5 multiply_convert_fusion
  194.6 3.2 add_convert_fusion.2
  198.8 3.7 multiply_convert_fusion.1
  202.5 4.2 multiply_convert_fusion.2
  216.1 2.4 fusion.191
  221.8 3.0 convolution_bitcast_fusion
  231.6 2.4 fusion.193
  235.5 2.1 multiply_reduce_fusion.7
  243.2 2.4 fusion.195
  247.2 2.3 pad_maximum_fusion.4
  252.6 2.6 fusion.5
  258.8 2.7 fusion.6
  267.7 2.4 fusion.17
  270.2 2.2 fusion.15
  272.4 2.3 fusion.16
  301.2 3.5 fusion.286
  304.7 2.8 fusion.282
  307.5 15.8 %reduce-scatter.17.cloned.1.call-done = f32[1,128,128]{1,2,0:T(8,128)} async-done(((f32[1,2048,128]{1,2,0:T(8,128)}), f32[1,128,128]{1,2,0:T(8,128)}) %reduce-scatter.17.cloned.1.call-update) | async-done | bytes 65552 | tf_op jit(solution)/shard_map/reduce_scatter | solution.py:246
  323.3 2.0 fusion.18
  325.3 75.0 %reduce-scatter.15.cloned.1.call-done = f32[1,128,128]{1,2,0:T(8,128)} async-done(((f32[1,2048,128]{1,2,0:T(8,128)}), f32[1,128,128]{1,2,0:T(8,128)}) %reduce-scatter.15.cloned.1.call-update) | async-done | bytes 65552 | tf_op jit(solution)/shard_map/reduce_scatter | solution.py:246
  402.3 75.0 %reduce-scatter.13.cloned.1.call-done = f32[1,128,128]{1,2,0:T(8,128)} async-done(((f32[1,2048,128]{1,2,0:T(8,128)}), f32[1,128,128]{1,2,0:T(8,128)}) %reduce-scatter.13.cloned.1.call-update) | async-done | bytes 65552 | tf_op jit(solution)/shard_map/reduce_scatter | solution.py:246
  477.3 3.0 fusion.99
  493.1 2.4 fusion.198
  497.1 39.5 %all-gather = bf16[2048,128]{1,0:T(8,128)(2,1)S(1)} all-gather(bf16[128,128]{1,0:T(8,128)(2,1)} %convolution_convert_fusion.11), channel_id=2, replica_groups=mesh['ctx'=16,'wsh'=2] {'ctx'}, dimensions={0}, use_global_device_ids=true | all-gather | bytes 557056 | tf_op jit(solution)/shard_map/all_gather | solution.py:188
  541.7 2.6 convolution_convert_fusion.3
  547.6 5.0 multiply_convert_fusion.3
  559.6 2.4 fusion.197
  564.7 2.2 convolution_bitcast_fusion.6
  582.4 2.3 fusion.14
  589.3 3.8 fusion.290
  593.2 53.5 %reduce-scatter.11.cloned.1.call-done = f32[1,128,128]{1,2,0:T(8,128)} async-done(((f32[1,2048,128]{1,2,0:T(8,128)}), f32[1,128,128]{1,2,0:T(8,128)}) %reduce-scatter.11.cloned.1.call-update) | async-done | bytes 65552 | tf_op jit(solution)/shard_map/reduce_scatter | solution.py:246
  651.8 7.0 add_convert_fusion.1
  660.7 2.3 fusion.29
  668.0 2.1 add_convert_fusion
  678.4 2.5 all-reduce.3
  683.6 3.4 reduce-scatter.23.cloned.1.call-done
  687.0 13.6 %reduce-scatter.27.cloned.1.call-done = bf16[256,2048]{1,0:T(8,128)(2,1)} async-done(((bf16[512,2048]{1,0:T(8,128)(2,1)}), bf16[256,2048]{1,0:T(8,128)(2,1)}) %reduce-scatter.27.cloned.1.call-update) | async-done | bytes 1048592 | tf_op jit(solution)/shard_map/reduce_scatter | solution.py:304
  700.7 13.6 %reduce-scatter.29.cloned.1.call-done = bf16[1024,512]{1,0:T(8,128)(2,1)} async-done(((bf16[2048,512]{1,0:T(8,128)(2,1)}), bf16[1024,512]{1,0:T(8,128)(2,1)}) %reduce-scatter.29.cloned.1.call-update) | async-done | bytes 1048592 | tf_op jit(solution)/shard_map/reduce_scatter | solution.py:307
  714.2 232.3 %all-reduce.5 = (f32[256]{0:T(256)}, f32[256,8]{0,1:T(8,128)}, f32[256,512]{1,0:T(8,128)}, f32[256,128]{1,0:T(8,128)}, f32[256,512]{1,0:T(8,128)}, /*index=5*/f3...) all-reduce(f32[256]{0:T(256)S(1)} %dynamic-slice_convert_fusion.1, ...), channel_id=1, replica_groups=mesh['ctx'=16,'wsh'=2] {'ctx'}, use_global_device_ids=true, to_apply=%region_77.78 | all-reduce | flops 1346048 | bytes 8077312 | tf_op jit(solution)/shard_map/psum | solution.py:311
  (687 shorter events, 185.2 us)
Async XLA Ops:
  7.2 10.6 %copy-start.102 = (bf16[256,128]{1,0:T(8,128)(2,1)S(1)}, bf16[256,128]{1,0:T(8,128)(2,1)}, u32[]{:S(2)}) copy-start(bf16[256,128]{1,0:T(8,128)(2,1)} %param.18) | copy-start | bytes 196612
  7.2 181.7 %all-gather.9.cloned.1.call-start = ((), (), s32[]{:S(2)}) async-start(), calls=%async_computation.10 | async-start | bytes 3145728 | tf_op jit(solution)/shard_map/all_gather | solution.py:145
  8.0 12.4 %copy-start.98 = (bf16[256,512]{1,0:T(8,128)(2,1)S(1)}, bf16[256,512]{1,0:T(8,128)(2,1)}, u32[]{:S(2)}) copy-start(bf16[256,512]{1,0:T(8,128)(2,1)} %param.17) | copy-start | bytes 786436
  8.0 186.6 %all-gather.11.cloned.1.call-start = ((), (), s32[]{:S(2)}) async-start(), calls=%async_computation.11 | async-start | bytes 3145728 | tf_op jit(solution)/shard_map/all_gather | solution.py:146
  8.7 314.6 %reduce-scatter.17.cloned.1.call-start = ((), (), s32[]{:S(2)}) async-start(), calls=%async_computation.15 | async-start | bytes 1114112 | tf_op jit(solution)/shard_map/reduce_scatter | solution.py:246
  10.9 9.2 copy-start.131
  11.7 11.7 %copy-start.180 = (f32[128]{0:T(128)}, f32[128]{0:T(128)S(1)}, u32[]{:S(2)}) copy-start(f32[128]{0:T(128)S(1)} %fusion.249) | copy-start | bytes 1540
  12.1 11.3 %copy-start.136 = (f32[128]{0:T(128)}, f32[128]{0:T(128)S(1)}, u32[]{:S(2)}) copy-start(f32[128]{0:T(128)S(1)} %fusion.251) | copy-start | bytes 1540
  12.2 11.2 %copy-start.183 = (f32[128]{0:T(128)}, f32[128]{0:T(128)S(1)}, u32[]{:S(2)}) copy-start(f32[128]{0:T(128)S(1)} %fusion.253) | copy-start | bytes 1540
  12.8 10.6 %copy-start.119 = (s32[128,2]{0,1:T(2,128)}, s32[128,2]{0,1:T(2,128)S(1)}, u32[]{:S(2)}) copy-start(s32[128,2]{0,1:T(2,128)S(1)} %get-tuple-element.384) | copy-start | bytes 3076
  12.8 11.8 %copy-start.118 = (s32[128,2]{0,1:T(2,128)}, s32[128,2]{0,1:T(2,128)S(1)}, u32[]{:S(2)}) copy-start(s32[128,2]{0,1:T(2,128)S(1)} %get-tuple-element.385) | copy-start | bytes 3076
  14.8 11.8 %copy-start.104 = (s32[128,2]{1,0:T(8,128)}, s32[128,2]{1,0:T(8,128)S(1)}, u32[]{:S(2)}) copy-start(s32[128,2]{1,0:T(8,128)S(1)} %copy.269) | copy-start | bytes 3076
  15.0 8.8 copy-start.28
  15.0 8.8 copy-start.32
  15.0 8.8 copy-start.34
  15.2 8.6 copy-start.111
  15.2 9.5 copy-start.161
  16.4 11.2 %copy-start.105 = (s32[128,2]{1,0:T(8,128)}, s32[128,2]{1,0:T(8,128)S(1)}, u32[]{:S(2)}) copy-start(s32[128,2]{1,0:T(8,128)S(1)} %copy.276) | copy-start | bytes 3076
  27.3 130.2 %copy-start.91 = (f32[128,2,64]{0,2,1:T(8,128)}, f32[128,2,64]{0,2,1:T(8,128)S(1)}, u32[]{:S(2)}) copy-start(f32[128,2,64]{0,2,1:T(8,128)S(1)} %copy.271) | copy-start | bytes 196612
  28.2 126.9 %copy-start.95 = (bf16[256,512]{1,0:T(8,128)(2,1)S(1)}, bf16[256,512]{1,0:T(8,128)(2,1)}, u32[]{:S(2)}) copy-start(bf16[256,512]{1,0:T(8,128)(2,1)} %param.19) | copy-start | bytes 786436
  75.7 86.4 %copy-start.44 = (bf16[2048,128]{1,0:T(8,128)(2,1)}, bf16[2048,128]{1,0:T(8,128)(2,1)S(1)}, u32[]{:S(2)}) copy-start(bf16[2048,128]{1,0:T(8,128)(2,1)S(1)} %all-gather.3) | copy-start | bytes 1572868
  114.3 44.3 %copy-start.40 = (bf16[2048,128]{1,0:T(8,128)(2,1)}, bf16[2048,128]{1,0:T(8,128)(2,1)S(1)}, u32[]{:S(2)}) copy-start(bf16[2048,128]{1,0:T(8,128)(2,1)S(1)} %all-gather.2) | copy-start | bytes 1572868
  114.3 43.8 %copy-start.93 = (f32[128,2,64]{0,2,1:T(8,128)S(1)}, f32[128,2,64]{0,2,1:T(8,128)}, u32[]{:S(2)}) copy-start(f32[128,2,64]{0,2,1:T(8,128)} %copy.285) | copy-start | bytes 196612
  167.1 9.2 copy-start.6
  167.1 9.2 copy-start.168
  183.1 11.4 %copy-start.18 = (f32[1,128,512]{2,1,0:T(8,128)}, f32[1,128,512]{2,1,0:T(8,128)S(1)}, u32[]{:S(2)}) copy-start(f32[1,128,512]{2,1,0:T(8,128)S(1)} %get-tuple-element.413) | copy-start | bytes 786436
  183.5 15.2 %copy-start.22 = (f32[1,128,512]{2,1,0:T(8,128)}, f32[1,128,512]{2,1,0:T(8,128)S(1)}, u32[]{:S(2)}) copy-start(f32[1,128,512]{2,1,0:T(8,128)S(1)} %get-tuple-element.408) | copy-start | bytes 786436
  183.5 15.2 %copy-start.145 = (f32[128]{0:T(128)}, f32[128]{0:T(128)S(1)}, u32[]{:S(2)}) copy-start(f32[128]{0:T(128)S(1)} %broadcast_multiply_fusion.7) | copy-start | bytes 1540
  183.9 10.6 %copy-start.15 = (f32[1,128,512]{2,1,0:T(8,128)}, f32[1,128,512]{2,1,0:T(8,128)S(1)}, u32[]{:S(2)}) copy-start(f32[1,128,512]{2,1,0:T(8,128)S(1)} %get-tuple-element.403) | copy-start | bytes 786436
  183.9 10.6 %copy-start.138 = (f32[128]{0:T(128)}, f32[128]{0:T(128)S(1)}, u32[]{:S(2)}) copy-start(f32[128]{0:T(128)S(1)} %broadcast_multiply_fusion.5) | copy-start | bytes 1540
  184.1 10.4 %copy-start.202 = (f32[128]{0:T(128)}, f32[128]{0:T(128)S(1)}, u32[]{:S(2)}) copy-start(f32[128]{0:T(128)S(1)} %multiply_reduce_fusion.2) | copy-start | bytes 1540
  184.3 10.2 %copy-start.200 = (f32[128]{0:T(128)}, f32[128]{0:T(128)S(1)}, u32[]{:S(2)}) copy-start(f32[128]{0:T(128)S(1)} %multiply_reduce_fusion.1) | copy-start | bytes 1540
  188.9 9.8 %copy-start.155 = (f32[128]{0:T(128)}, f32[128]{0:T(128)S(1)}, u32[]{:S(2)}) copy-start(f32[128]{0:T(128)S(1)} %fusion.252) | copy-start | bytes 1540
  249.5 150.9 %reduce-scatter.15.cloned.1.call-start = ((), (), s32[]{:S(2)}) async-start(), calls=%async_computation.14 | async-start | bytes 1114112 | tf_op jit(solution)/shard_map/reduce_scatter | solution.py:246
  265.1 9.5 copy-start.51
  265.1 9.5 copy-start.90
  276.7 200.6 %reduce-scatter.13.cloned.1.call-start = ((), (), s32[]{:S(2)}) async-start(), calls=%async_computation.13 | async-start | bytes 1114112 | tf_op jit(solution)/shard_map/reduce_scatter | solution.py:246
  294.6 352.0 %reduce-scatter.11.cloned.1.call-start = ((), (), s32[]{:S(2)}) async-start(), calls=%async_computation.12 | async-start | bytes 1114112 | tf_op jit(solution)/shard_map/reduce_scatter | solution.py:246
  571.8 103.9 %reduce-scatter.19.cloned.1.call-start = ((), (), s32[]{:S(2)}) async-start(), calls=%async_computation.16 | async-start | bytes 12288 | tf_op jit(solution)/shard_map/reduce_scatter | solution.py:289
  582.1 93.6 %reduce-scatter.25.cloned.1.call-start = ((), (), s32[]{:S(2)}) async-start(), calls=%async_computation.19 | async-start | bytes 786432 | tf_op jit(solution)/shard_map/reduce_scatter | solution.py:298
  585.8 90.5 %reduce-scatter.21.cloned.1.call-start = ((), (), s32[]{:S(2)}) async-start(), calls=%async_computation.17 | async-start | bytes 786432 | tf_op jit(solution)/shard_map/reduce_scatter | solution.py:292
  589.2 97.8 %reduce-scatter.23.cloned.1.call-start = ((), (), s32[]{:S(2)}) async-start(), calls=%async_computation.18 | async-start | bytes 196608 | tf_op jit(solution)/shard_map/reduce_scatter | solution.py:295
  593.2 58.6 %copy-start.17 = (f32[1,128,512]{2,1,0:T(8,128)S(1)}, f32[1,128,512]{2,1,0:T(8,128)}, u32[]{:S(2)}) copy-start(f32[1,128,512]{2,1,0:T(8,128)} %copy-done.15) | copy-start | bytes 786436
  651.7 48.9 %reduce-scatter.27.cloned.1.call-start = ((), (), s32[]{:S(2)}) async-start(), calls=%async_computation.20 | async-start | bytes 3145728 | tf_op jit(solution)/shard_map/reduce_scatter | solution.py:304
  658.8 55.4 %reduce-scatter.29.cloned.1.call-start = ((), (), s32[]{:S(2)}) async-start(), calls=%async_computation.21 | async-start | bytes 3145728 | tf_op jit(solution)/shard_map/reduce_scatter | solution.py:307
  682.2 32.0 %copy-start.96 = (bf16[256,512]{1,0:T(8,128)(2,1)S(1)}, bf16[256,512]{1,0:T(8,128)(2,1)}, u32[]{:S(2)}) copy-start(bf16[256,512]{1,0:T(8,128)(2,1)} %reduce-scatter.25.cloned.1.call-done) | copy-start | bytes 786436
  682.2 32.0 %copy-start.97 = (bf16[256,512]{1,0:T(8,128)(2,1)S(1)}, bf16[256,512]{1,0:T(8,128)(2,1)}, u32[]{:S(2)}) copy-start(bf16[256,512]{1,0:T(8,128)(2,1)} %reduce-scatter.21.cloned.1.call-done) | copy-start | bytes 786436
  682.2 32.0 %copy-start.167 = (bf16[256,8]{0,1:T(8,128)(2,1)S(1)}, bf16[256,8]{0,1:T(8,128)(2,1)}, u32[]{:S(2)}) copy-start(bf16[256,8]{0,1:T(8,128)(2,1)} %reduce-scatter.19.cloned.1.call-done) | copy-start | bytes 12292
  (175 other events, 585.2 us)
Sparse Core Ops, SparseCore 0:
  9.6 13.6 all-gather.8
  24.8 11.3 all-gather.10
  249.6 73.6 reduce-scatter.16
  326.1 74.1 reduce-scatter.14
  403.0 74.2 reduce-scatter.12
  571.9 74.7 reduce-scatter.10
  649.4 3.9 reduce-scatter.18
  655.6 9.1 reduce-scatter.24
  667.2 9.0 reduce-scatter.20
  678.4 8.6 reduce-scatter.22
  689.9 10.7 reduce-scatter.26
  703.4 10.7 reduce-scatter.28
where the time goes:
time: 961 us; the launch traced here: 954 us
  blocking collectives  411 us (43%)
  waiting for transfers between devices  252 us (26%)
  matrix products  171 us (18%)
  local copies, waits for them, and re-layouts  55.3 us (6%)
  other arithmetic  44.9 us (5%)
  between operations  18.1 us (2%)
    psum x1, blocking collectives, on_device(): lax.psum((owned[0], owned[1], owned[2], owned[3], owned[4], owned[5], own...  232 us
    reduce_scatter x4, waiting for transfers between devices, on_device(): own_kv = lax.psum_scatter(full_kv, 'ctx', scatter_dimension=1, tiled=True)  219 us
    all_gather x4, blocking collectives, on_device(): kv_all = lax.all_gather(keyval, 'ctx', axis=1, tiled=True)  164 us
  transfers between devices with their start and end apart: 12, of which 8 were waited for; matrix products, arithmetic and copies ran while one was open for 16% of the time, Pallas kernels for 0%

commit v1 on v0

--- a/solution.py
+++ b/solution.py
@@ -185,7 +185,14 @@
         keyval = jnp.dot(normed_low, kv_mat, preferred_element_type=jnp.float32).astype(
             jnp.bfloat16
         )
-        kv_all = lax.all_gather(keyval, "ctx", axis=1, tiled=True)
+        piece_now, o_now = (lax.axis_size("ctx"), lax.axis_index("ctx"))
+        kv_all, z1 = (keyval, 1)
+        while z1 < piece_now:
+            y = lax.ppermute(kv_all, "ctx", [(idx, idx ^ z1) for idx in range(piece_now)])
+            before = jnp.concatenate([kv_all, y], 1)
+            x_new = jnp.concatenate([y, kv_all], 1)
+            kv_all = jnp.where(o_now & z1 == 0, before, x_new)
+            z1 = 2 * z1
         log_total = log_totals(queries, kv_all, query_places, key_places)
         attended = attend(queries, kv_all, query_places, key_places, log_total)
         weighted = gate_values[..., None] * attended

time: 961 us -> 874 us (0.909)
  blocking collectives: 411 us -> 247 us
  waiting for transfers between devices: 252 us -> 295 us
  other arithmetic: 44.9 us -> 63.3 us
  starting transfers between devices: 0.92 us -> 18.4 us
    all_gather x4 -> x0, blocking collectives: 164 us -> none  [on_device(): kv_all = lax.all_gather(keyval, 'ctx', axis=1, tiled=True)]
    ppermute x0 -> x16, waiting for transfers between devices: none -> 43 us  [on_device(): lax.ppermute(kv_all, 'ctx', [(idx, idx ^ z1) for idx in range(piece_now)])]
    ppermute x0 -> x16, starting transfers between devices: none -> 17.3 us  [on_device(): lax.ppermute(kv_all, 'ctx', [(idx, idx ^ z1) for idx in range(piece_now)])]
  transfers between devices with their start and end apart: 12 -> 28, of which waited for: 8 -> 15; matrix products, arithmetic and copies ran while one was open for 16% -> 21% of each run, Pallas kernels for 0% -> 0%
where the time goes in v1:
time: 874 us; the launch traced here: 866 us
  waiting for transfers between devices  295 us (34%)
  blocking collectives  247 us (28%)
  matrix products  170 us (19%)
  other arithmetic  63.3 us (7%)
  local copies, waits for them, and re-layouts  54.5 us (6%)
  starting transfers between devices  18.4 us (2%)
  between operations  18.1 us (2%)
    psum x1, blocking collectives, on_device(): lax.psum((owned[0], owned[1], owned[2], owned[3], owned[4], owned[5], own...  232 us
    reduce_scatter x4, waiting for transfers between devices, on_device(): own_kv = lax.psum_scatter(full_kv, 'ctx', scatter_dimension=1, tiled=True)  224 us
    ppermute x16, waiting for transfers between devices, on_device(): lax.ppermute(kv_all, 'ctx', [(idx, idx ^ z1) for idx in range(piece_now)])  43 us
    dot_general x4, matrix products, on_device(): jnp.dot(normed_two_low, up_mat, preferred_element_type=jnp.float32)  18.4 us
  transfers between devices with their start and end apart: 28, of which 15 were waited for; matrix products, arithmetic and copies ran while one was open for 21% of the time, Pallas kernels for 0%

profile of v1, /device:TPU:0, one launch (start us, length us, event | category | flops | bytes accessed | tf_op | source)
XLA Modules:
  0.0 865.8 jit_solution(11327016094311856697)
XLA Ops:
  11.9 2.1 all_gather.27
  16.4 2.9 collective-permute-start.12
  19.7 2.1 collective-permute-start.4
  29.6 2.2 all_gather.26
  37.3 2.2 all_gather.28
  57.9 2.7 collective-permute-start.15
  60.5 6.4 collective-permute-done.6
  70.4 20.1 %collective-permute-done.7 = bf16[1,1024,128]{2,1,0:T(8,128)(2,1)S(1)} collective-permute-done((bf16[1,1024,128]{2,1,0:T(8,128)(2,1)S(1)}, bf16[1,1024,128]{2,1,0:T(8,128)(2,1)S(1)}, u32[]{:S(2)}, u32[]{:S(2)}) %collective-permute-start.7) | collective-permute-done | bytes 262176 | tf_op jit(solution)/shard_map/ppermute | solution.py:191
  99.7 2.5 convolution_convert_fusion
  102.2 3.2 broadcast_multiply_fusion.1
  107.0 2.6 convolution_convert_fusion.1
  111.3 2.5 broadcast_multiply_fusion.2
  120.3 5.9 multiply_convert_fusion
  126.3 3.2 add_convert_fusion.2
  130.5 3.7 multiply_convert_fusion.1
  134.2 3.7 multiply_convert_fusion.2
  147.4 2.4 fusion.195
  153.0 3.0 convolution_bitcast_fusion
  162.8 2.3 fusion.197
  174.4 2.4 fusion.199
  178.4 2.3 pad_maximum_fusion.4
  183.9 2.6 fusion.5
  190.1 2.7 fusion.6
  199.0 2.4 fusion.17
  201.4 2.3 fusion.15
  203.7 2.3 fusion.16
  232.7 3.5 fusion.290
  236.2 2.8 fusion.286
  239.0 19.0 %reduce-scatter.17.cloned.1.call-done = f32[1,128,128]{1,2,0:T(8,128)} async-done(((f32[1,2048,128]{1,2,0:T(8,128)}), f32[1,128,128]{1,2,0:T(8,128)}) %reduce-scatter.17.cloned.1.call-update) | async-done | bytes 65552 | tf_op jit(solution)/shard_map/reduce_scatter | solution.py:253
  259.9 75.0 %reduce-scatter.15.cloned.1.call-done = f32[1,128,128]{1,2,0:T(8,128)} async-done(((f32[1,2048,128]{1,2,0:T(8,128)}), f32[1,128,128]{1,2,0:T(8,128)}) %reduce-scatter.15.cloned.1.call-update) | async-done | bytes 65552 | tf_op jit(solution)/shard_map/reduce_scatter | solution.py:253
  336.9 74.9 %reduce-scatter.13.cloned.1.call-done = f32[1,128,128]{1,2,0:T(8,128)} async-done(((f32[1,2048,128]{1,2,0:T(8,128)}), f32[1,128,128]{1,2,0:T(8,128)}) %reduce-scatter.13.cloned.1.call-update) | async-done | bytes 65552 | tf_op jit(solution)/shard_map/reduce_scatter | solution.py:253
  411.7 3.0 fusion.99
  422.7 2.4 fusion.202
  427.6 3.4 collective-permute-done.1
  440.4 7.8 collective-permute-done.3
  452.6 2.6 convolution_convert_fusion.3
  458.5 5.0 multiply_convert_fusion.3
  470.5 2.7 fusion.201
  475.9 2.2 convolution_bitcast_fusion.6
  493.3 2.3 fusion.14
  500.2 3.8 fusion.294
  504.1 54.7 %reduce-scatter.11.cloned.1.call-done = f32[1,128,128]{1,2,0:T(8,128)} async-done(((f32[1,2048,128]{1,2,0:T(8,128)}), f32[1,128,128]{1,2,0:T(8,128)}) %reduce-scatter.11.cloned.1.call-update) | async-done | bytes 65552 | tf_op jit(solution)/shard_map/reduce_scatter | solution.py:253
  563.9 7.0 add_convert_fusion.1
  572.8 2.3 fusion.29
  592.5 2.6 all-reduce.3
  599.1 13.5 %reduce-scatter.27.cloned.1.call-done = bf16[256,2048]{1,0:T(8,128)(2,1)} async-done(((bf16[512,2048]{1,0:T(8,128)(2,1)}), bf16[256,2048]{1,0:T(8,128)(2,1)}) %reduce-scatter.27.cloned.1.call-update) | async-done | bytes 1048592 | tf_op jit(solution)/shard_map/reduce_scatter | solution.py:311
  612.6 13.6 %reduce-scatter.29.cloned.1.call-done = bf16[1024,512]{1,0:T(8,128)(2,1)} async-done(((bf16[2048,512]{1,0:T(8,128)(2,1)}), bf16[1024,512]{1,0:T(8,128)(2,1)}) %reduce-scatter.29.cloned.1.call-update) | async-done | bytes 1048592 | tf_op jit(solution)/shard_map/reduce_scatter | solution.py:314
  626.2 232.2 %all-reduce.5 = (f32[256]{0:T(256)}, f32[256,8]{0,1:T(8,128)}, f32[256,512]{1,0:T(8,128)}, f32[256,128]{1,0:T(8,128)}, f32[256,512]{1,0:T(8,128)}, /*index=5*/f3...) all-reduce(f32[256]{0:T(256)S(1)} %dynamic-slice_convert_fusion.1, ...), channel_id=1, replica_groups=mesh['ctx'=16,'wsh'=2] {'ctx'}, use_global_device_ids=true, to_apply=%region_77.78 | all-reduce | flops 1346048 | bytes 8077312 | tf_op jit(solution)/shard_map/psum | solution.py:318
  (707 shorter events, 219.0 us)
Async XLA Ops:
  7.2 113.1 %all-gather.5.cloned.1.call-start = ((), (), s32[]{:S(2)}) async-start(), calls=%async_computation.10 | async-start | bytes 3145728 | tf_op jit(solution)/shard_map/all_gather | solution.py:145
  7.9 14.0 %copy-start.168 = (s32[4,128,2]{1,2,0:T(2,128)S(1)}, s32[4,128,2]{1,2,0:T(2,128)}, u32[]{:S(2)}) copy-start(s32[4,128,2]{1,2,0:T(2,128)} %param.13) | copy-start | bytes 12292
  7.9 14.5 %copy-start.167 = (bf16[256,8]{0,1:T(8,128)(2,1)S(1)}, bf16[256,8]{0,1:T(8,128)(2,1)}, u32[]{:S(2)}) copy-start(bf16[256,8]{0,1:T(8,128)(2,1)} %param.16) | copy-start | bytes 12292
  7.9 118.4 %all-gather.7.cloned.1.call-start = ((), (), s32[]{:S(2)}) async-start(), calls=%async_computation.11 | async-start | bytes 3145728 | tf_op jit(solution)/shard_map/all_gather | solution.py:146
  9.2 15.2 %copy-start.130 = (f32[128]{0:T(128)}, f32[128]{0:T(128)S(1)}, u32[]{:S(2)}) copy-start(f32[128]{0:T(128)S(1)} %broadcast_multiply_fusion.10) | copy-start | bytes 1540
  9.9 19.6 %copy-start.102 = (bf16[256,512]{1,0:T(8,128)(2,1)S(1)}, bf16[256,512]{1,0:T(8,128)(2,1)}, u32[]{:S(2)}) copy-start(bf16[256,512]{1,0:T(8,128)(2,1)} %param.17) | copy-start | bytes 786436
  15.4 16.4 %copy-start.179 = (f32[128]{0:T(128)}, f32[128]{0:T(128)S(1)}, u32[]{:S(2)}) copy-start(f32[128]{0:T(128)S(1)} %get-tuple-element.268) | copy-start | bytes 1540
  16.0 15.8 %copy-start.175 = (f32[128]{0:T(128)}, f32[128]{0:T(128)S(1)}, u32[]{:S(2)}) copy-start(f32[128]{0:T(128)S(1)} %fusion.257) | copy-start | bytes 1540
  16.2 15.9 %copy-start.32 = (bf16[1,128,512]{2,1,0:T(8,128)(2,1)}, bf16[1,128,512]{2,1,0:T(8,128)(2,1)S(1)}, u32[]{:S(2)}) copy-start(bf16[1,128,512]{2,1,0:T(8,128)(2,1)S(1)} %get-tuple-element.368) | copy-start | bytes 393220
  16.2 15.9 %copy-start.34 = (bf16[1,128,512]{2,1,0:T(8,128)(2,1)}, bf16[1,128,512]{2,1,0:T(8,128)(2,1)S(1)}, u32[]{:S(2)}) copy-start(bf16[1,128,512]{2,1,0:T(8,128)(2,1)S(1)} %get-tuple-element.367) | copy-start | bytes 393220
  16.2 16.2 %copy-start.28 = (bf16[1,128,512]{2,1,0:T(8,128)(2,1)}, bf16[1,128,512]{2,1,0:T(8,128)(2,1)S(1)}, u32[]{:S(2)}) copy-start(bf16[1,128,512]{2,1,0:T(8,128)(2,1)S(1)} %get-tuple-element.369) | copy-start | bytes 393220
  16.4 30.4 %collective-permute-start.12 = (bf16[1,128,128]{2,1,0:T(8,128)(2,1)S(1)}, bf16[1,128,128]{2,1,0:T(8,128)(2,1)S(1)}, u32[]{:S(2)}, u32[]{:S(2)}) collective-permute-start(bf16[1,128,128]{2,1,0:T(8,128)(2,1)S(1)} %bitcast.578), channel_id=1, source_target_pairs={{0,2},{2,0},{4,6},{6,4},{8,10},{10,8},{12,14},{14,12},{16,18},{18,... | collective-permute-start | bytes 98312 | tf_op jit(solution)/shard_map/ppermute | solution.py:191
  19.5 26.5 %collective-permute-start.8 = (bf16[1,128,128]{2,1,0:T(8,128)(2,1)S(1)}, bf16[1,128,128]{2,1,0:T(8,128)(2,1)}, u32[]{:S(2)}, u32[]{:S(2)}) collective-permute-start(bf16[1,128,128]{2,1,0:T(8,128)(2,1)S(1)} %bitcast.582), channel_id=1, source_target_pairs={{0,2},{2,0},{4,6},{6,4},{8,10},{10,8},{12,14},{14,12},{16,18},{18,... | collective-permute-start | bytes 98312 | tf_op jit(solution)/shard_map/ppermute | solution.py:191
  19.7 25.4 %collective-permute-start.4 = (bf16[1,128,128]{2,1,0:T(8,128)(2,1)S(1)}, bf16[1,128,128]{2,1,0:T(8,128)(2,1)}, u32[]{:S(2)}, u32[]{:S(2)}) collective-permute-start(bf16[1,128,128]{2,1,0:T(8,128)(2,1)S(1)} %bitcast.580), channel_id=1, source_target_pairs={{0,2},{2,0},{4,6},{6,4},{8,10},{10,8},{12,14},{14,12},{16,18},{18,... | collective-permute-start | bytes 98312 | tf_op jit(solution)/shard_map/ppermute | solution.py:191
  21.8 236.1 %reduce-scatter.17.cloned.1.call-start = ((), (), s32[]{:S(2)}) async-start(), calls=%async_computation.15 | async-start | bytes 1114112 | tf_op jit(solution)/shard_map/reduce_scatter | solution.py:253
  22.5 10.2 %copy-start.118 = (s32[128,2]{0,1:T(2,128)}, s32[128,2]{0,1:T(2,128)S(1)}, u32[]{:S(2)}) copy-start(s32[128,2]{0,1:T(2,128)S(1)} %get-tuple-element.385) | copy-start | bytes 3076
  22.5 10.3 %copy-start.120 = (s32[128,2]{0,1:T(2,128)}, s32[128,2]{0,1:T(2,128)S(1)}, u32[]{:S(2)}) copy-start(s32[128,2]{0,1:T(2,128)S(1)} %get-tuple-element.386) | copy-start | bytes 3076
  43.7 47.0 %copy-start.92 = (f32[128,2,64]{0,2,1:T(8,128)}, f32[128,2,64]{0,2,1:T(8,128)S(1)}, u32[]{:S(2)}) copy-start(f32[128,2,64]{0,2,1:T(8,128)S(1)} %copy.271) | copy-start | bytes 196612
  46.9 5.5 collective-permute-start.13
  49.3 7.5 collective-permute-start.9
  50.7 4.3 collective-permute-start.5
  52.4 5.3 collective-permute-start.14
  55.2 11.8 %collective-permute-start.6 = (bf16[1,512,128]{2,1,0:T(8,128)(2,1)S(1)}, bf16[1,512,128]{2,1,0:T(8,128)(2,1)S(1)}, u32[]{:S(2)}, u32[]{:S(2)}) collective-permute-start(bf16[1,512,128]{2,1,0:T(8,128)(2,1)S(1)} %maximum_select_fusion.15), channel_id=1, source_target_pairs={{0,8},{2,10},{4,12},{6,14},{8,0},{10,2},{12,4},{14,6},{16,24},{18,... | collective-permute-start | bytes 393224 | tf_op jit(solution)/shard_map/ppermute | solution.py:191
  56.9 11.4 %collective-permute-start.10 = (bf16[1,512,128]{2,1,0:T(8,128)(2,1)S(1)}, bf16[1,512,128]{2,1,0:T(8,128)(2,1)S(1)}, u32[]{:S(2)}, u32[]{:S(2)}) collective-permute-start(bf16[1,512,128]{2,1,0:T(8,128)(2,1)S(1)} %maximum_select_fusion.17), channel_id=1, source_target_pairs={{0,8},{2,10},{4,12},{6,14},{8,0},{10,2},{12,4},{14,6},{16,24},{18,... | collective-permute-start | bytes 393224 | tf_op jit(solution)/shard_map/ppermute | solution.py:191
  57.9 33.5 %collective-permute-start.15 = (bf16[1,1024,128]{2,1,0:T(8,128)(2,1)S(1)}, bf16[1,1024,128]{2,1,0:T(8,128)(2,1)S(1)}, u32[]{:S(2)}, u32[]{:S(2)}) collective-permute-start(bf16[1,1024,128]{2,1,0:T(8,128)(2,1)S(1)} %maximum_select_fusion.11), channel_id=1, source_target_pairs={{0,16},{2,18},{4,20},{6,22},{8,24},{10,26},{12,28},{14,30},{16,0},... | collective-permute-start | bytes 786440 | tf_op jit(solution)/shard_map/ppermute | solution.py:191
  67.0 23.5 %collective-permute-start.7 = (bf16[1,1024,128]{2,1,0:T(8,128)(2,1)S(1)}, bf16[1,1024,128]{2,1,0:T(8,128)(2,1)S(1)}, u32[]{:S(2)}, u32[]{:S(2)}) collective-permute-start(bf16[1,1024,128]{2,1,0:T(8,128)(2,1)S(1)} %maximum_select_fusion.7), channel_id=1, source_target_pairs={{0,16},{2,18},{4,20},{6,22},{8,24},{10,26},{12,28},{14,30},{16,0},... | collective-permute-start | bytes 786440 | tf_op jit(solution)/shard_map/ppermute | solution.py:191
  68.4 25.2 %collective-permute-start.11 = (bf16[1,1024,128]{2,1,0:T(8,128)(2,1)S(1)}, bf16[1,1024,128]{2,1,0:T(8,128)(2,1)S(1)}, u32[]{:S(2)}, u32[]{:S(2)}) collective-permute-start(bf16[1,1024,128]{2,1,0:T(8,128)(2,1)S(1)} %maximum_select_fusion.9), channel_id=1, source_target_pairs={{0,16},{2,18},{4,20},{6,22},{8,24},{10,26},{12,28},{14,30},{16,0},... | collective-permute-start | bytes 786440 | tf_op jit(solution)/shard_map/ppermute | solution.py:191
  118.5 11.9 %copy-start.22 = (f32[1,128,512]{2,1,0:T(8,128)}, f32[1,128,512]{2,1,0:T(8,128)S(1)}, u32[]{:S(2)}) copy-start(f32[1,128,512]{2,1,0:T(8,128)S(1)} %get-tuple-element.408) | copy-start | bytes 786436
  118.5 11.9 %copy-start.140 = (f32[128]{0:T(128)}, f32[128]{0:T(128)S(1)}, u32[]{:S(2)}) copy-start(f32[128]{0:T(128)S(1)} %broadcast_multiply_fusion.7) | copy-start | bytes 1540
  120.2 10.2 %copy-start.150 = (f32[128]{0:T(128)}, f32[128]{0:T(128)S(1)}, u32[]{:S(2)}) copy-start(f32[128]{0:T(128)S(1)} %fusion.256) | copy-start | bytes 1540
  180.7 154.2 %reduce-scatter.15.cloned.1.call-start = ((), (), s32[]{:S(2)}) async-start(), calls=%async_computation.14 | async-start | bytes 1114112 | tf_op jit(solution)/shard_map/reduce_scatter | solution.py:253
  208.0 203.7 %reduce-scatter.13.cloned.1.call-start = ((), (), s32[]{:S(2)}) async-start(), calls=%async_computation.13 | async-start | bytes 1114112 | tf_op jit(solution)/shard_map/reduce_scatter | solution.py:253
  225.9 332.9 %reduce-scatter.11.cloned.1.call-start = ((), (), s32[]{:S(2)}) async-start(), calls=%async_computation.12 | async-start | bytes 1114112 | tf_op jit(solution)/shard_map/reduce_scatter | solution.py:253
  420.7 5.0 collective-permute-start
  426.6 4.3 collective-permute-start.1
  431.7 5.3 collective-permute-start.2
  434.6 13.7 %copy-start.93 = (f32[128,2,64]{0,2,1:T(8,128)S(1)}, f32[128,2,64]{0,2,1:T(8,128)}, u32[]{:S(2)}) copy-start(f32[128,2,64]{0,2,1:T(8,128)} %copy.264) | copy-start | bytes 196612
  438.0 10.1 %collective-permute-start.3 = (bf16[1,1024,128]{2,1,0:T(8,128)(2,1)S(1)}, bf16[1,1024,128]{2,1,0:T(8,128)(2,1)S(1)}, u32[]{:S(2)}, u32[]{:S(2)}) collective-permute-start(bf16[1,1024,128]{2,1,0:T(8,128)(2,1)S(1)} %maximum_select_fusion.5), channel_id=1, source_target_pairs={{0,16},{2,18},{4,20},{6,22},{8,24},{10,26},{12,28},{14,30},{16,0},... | collective-permute-start | bytes 786440 | tf_op jit(solution)/shard_map/ppermute | solution.py:191
  482.9 105.7 %reduce-scatter.19.cloned.1.call-start = ((), (), s32[]{:S(2)}) async-start(), calls=%async_computation.16 | async-start | bytes 12288 | tf_op jit(solution)/shard_map/reduce_scatter | solution.py:296
  493.3 95.4 %reduce-scatter.25.cloned.1.call-start = ((), (), s32[]{:S(2)}) async-start(), calls=%async_computation.19 | async-start | bytes 786432 | tf_op jit(solution)/shard_map/reduce_scatter | solution.py:305
  496.7 91.9 %reduce-scatter.21.cloned.1.call-start = ((), (), s32[]{:S(2)}) async-start(), calls=%async_computation.17 | async-start | bytes 786432 | tf_op jit(solution)/shard_map/reduce_scatter | solution.py:299
  500.1 98.9 %reduce-scatter.23.cloned.1.call-start = ((), (), s32[]{:S(2)}) async-start(), calls=%async_computation.18 | async-start | bytes 196608 | tf_op jit(solution)/shard_map/reduce_scatter | solution.py:302
  504.0 59.8 %copy-start.17 = (f32[1,128,512]{2,1,0:T(8,128)S(1)}, f32[1,128,512]{2,1,0:T(8,128)}, u32[]{:S(2)}) copy-start(f32[1,128,512]{2,1,0:T(8,128)} %copy-done.15) | copy-start | bytes 786436
  563.8 48.8 %reduce-scatter.27.cloned.1.call-start = ((), (), s32[]{:S(2)}) async-start(), calls=%async_computation.20 | async-start | bytes 3145728 | tf_op jit(solution)/shard_map/reduce_scatter | solution.py:311
  570.9 55.2 %reduce-scatter.29.cloned.1.call-start = ((), (), s32[]{:S(2)}) async-start(), calls=%async_computation.21 | async-start | bytes 3145728 | tf_op jit(solution)/shard_map/reduce_scatter | solution.py:314
  597.7 28.5 %copy-start.99 = (bf16[256,512]{1,0:T(8,128)(2,1)S(1)}, bf16[256,512]{1,0:T(8,128)(2,1)}, u32[]{:S(2)}) copy-start(bf16[256,512]{1,0:T(8,128)(2,1)} %reduce-scatter.25.cloned.1.call-done) | copy-start | bytes 786436
  597.7 28.5 %copy-start.100 = (bf16[256,512]{1,0:T(8,128)(2,1)S(1)}, bf16[256,512]{1,0:T(8,128)(2,1)}, u32[]{:S(2)}) copy-start(bf16[256,512]{1,0:T(8,128)(2,1)} %reduce-scatter.21.cloned.1.call-done) | copy-start | bytes 786436
  597.7 28.5 %copy-start.161 = (bf16[256,8]{0,1:T(8,128)(2,1)S(1)}, bf16[256,8]{0,1:T(8,128)(2,1)}, u32[]{:S(2)}) copy-start(bf16[256,8]{0,1:T(8,128)(2,1)} %reduce-scatter.19.cloned.1.call-done) | copy-start | bytes 12292
  (173 other events, 668.3 us)
Sparse Core Ops, SparseCore 0:
  9.6 13.2 all-gather.4
  24.4 11.7 all-gather.6
  180.8 77.0 reduce-scatter.16
  260.7 74.1 reduce-scatter.14
  337.6 74.1 reduce-scatter.12
  483.0 75.6 reduce-scatter.10
  561.5 3.7 reduce-scatter.18
  567.6 9.1 reduce-scatter.24
  579.1 9.0 reduce-scatter.20
  590.3 8.6 reduce-scatter.22
  601.8 10.7 reduce-scatter.26
  615.4 10.7 reduce-scatter.28
